TPU v7x, 32 devices: a whole 2x2x4 slice. The times are simulated.
32 devices in a mesh: blk: 4 (over x, core), uly: 8 (over z, y).
Axes of the slice: x: 2, y: 2, z: 4, core: 2. Of those that a mesh axis runs over, the one named last changes fastest.
Arguments:
- query_rows: bfloat16 [4096, 512], P(('blk', 'uly')), may hold values from -6 to 6
- key_rows: bfloat16 [4096, 512], P(('blk', 'uly')), may hold values from -6 to 6
- value_rows: bfloat16 [4096, 512], P(('blk', 'uly')), may hold values from -6 to 6
- out_grad: bfloat16 [4096, 512], P(('blk', 'uly')), may hold values from -6 to 6
- block_lists: int32 [64, 8], P('blk'), may hold values from 0 to 63, as said below
- block_counts: int32 [64], P('blk'), may hold values from 1 to 8
Outputs:
- attended: bfloat16 [4096, 512], P(('blk', 'uly'))
- query_gradient: bfloat16 [4096, 512], P(('blk', 'uly'))
- key_grad: bfloat16 [4096, 512], P(('blk', 'uly'))
- value_grad: bfloat16 [4096, 512], P(('blk', 'uly'))
Inputs may be any that keep to these rules, and one draw needn't show every extreme that they name: `block_lists`: row b lists key blocks of query block b: entry 0 is b, entries 1 to block_counts[b] - 1 are distinct blocks other than b, and the remaining entries equal b.
All inputs are finite; a program needn't handle non-finite values.
Results may differ from a plain program's by a relative error of at most 0.02.
Values may be sent and summed in bfloat16 or wider, within the bound.
A program may use at most 128 MiB of HBM per device.

v0:
```python
import math

import jax
import jax.numpy as jnp
from jax import lax
from jax.sharding import PartitionSpec as P

HDIM = 64
BLK = 64
KSEL = 8


def fetch_sets(pair_blocks, list_group, count_group):
    picked = pair_blocks[list_group]
    usable = (jnp.arange(KSEL)[None, :] < count_group[:, None])[:, None, None, :, None]
    return (picked[..., :HDIM], picked[..., HDIM:], usable)


def probabilities(query_group, gathered_key_blocks, usable):
    logit_matrix = jnp.einsum(
        "gqhd,gjkhd->gqhjk", query_group, gathered_key_blocks, preferred_element_type=jnp.float32
    ) * (1.0 / math.sqrt(HDIM))
    row_max = jnp.max(jnp.where(usable, logit_matrix, -1e30), axis=(3, 4), keepdims=True)
    weights = jnp.where(usable, jnp.exp(logit_matrix - row_max), 0.0)
    return weights / jnp.sum(weights, axis=(3, 4), keepdims=True)


def attend(reduced_precision, gathered_value_blocks):
    return jnp.einsum(
        "gqhjk,gjkhd->gqhd",
        reduced_precision,
        gathered_value_blocks,
        preferred_element_type=jnp.float32,
    ).astype(jnp.bfloat16)


def backward_group(
    gathered_key_blocks,
    gathered_value_blocks,
    query_group,
    grad_group,
    out_group,
    probability,
    reduced_precision,
):
    softmax_scale = 1.0 / math.sqrt(HDIM)
    delta = jnp.sum(grad_group.astype(jnp.float32) * out_group.astype(jnp.float32), axis=-1)[
        ..., None, None
    ]
    probability_gradient = jnp.einsum(
        "gqhd,gjkhd->gqhjk", grad_group, gathered_value_blocks, preferred_element_type=jnp.float32
    )
    score_gradient = (probability * (probability_gradient - delta)).astype(jnp.bfloat16)
    query_gradient = (
        jnp.einsum(
            "gqhjk,gjkhd->gqhd",
            score_gradient,
            gathered_key_blocks,
            preferred_element_type=jnp.float32,
        )
        * softmax_scale
    ).astype(jnp.bfloat16)
    key_contribution = (
        jnp.einsum(
            "gqhjk,gqhd->gjkhd", score_gradient, query_group, preferred_element_type=jnp.float32
        )
        * softmax_scale
    )
    value_contribution = jnp.einsum(
        "gqhjk,gqhd->gjkhd", reduced_precision, grad_group, preferred_element_type=jnp.float32
    )
    return (query_gradient, jnp.concatenate([key_contribution, value_contribution], axis=-1))


def on_device(query_rows, key_rows, value_rows, out_grad, block_lists, block_counts):
    tok_rows = query_rows.shape[0]
    width = query_rows.shape[1]
    heads = width // HDIM
    query_heads = query_rows.reshape(tok_rows, heads, HDIM)
    grad_heads = out_grad.reshape(tok_rows, heads, HDIM)
    pair_heads = jnp.concatenate(
        [key_rows.reshape(tok_rows, heads, HDIM), value_rows.reshape(tok_rows, heads, HDIM)], axis=2
    )
    seg_query, seg_pair, seg_grad = (
        lax.all_to_all(query_heads, "uly", split_axis=1, concat_axis=0, tiled=True),
        lax.all_to_all(pair_heads, "uly", split_axis=1, concat_axis=0, tiled=True),
        lax.all_to_all(grad_heads, "uly", split_axis=1, concat_axis=0, tiled=True),
    )
    all_pairs = lax.all_gather(seg_pair, "blk", axis=0, tiled=True)
    seg_rows = seg_query.shape[0]
    head_local = seg_query.shape[1]
    local_blocks = seg_rows // BLK
    group_size = math.gcd(16, local_blocks)
    groups = local_blocks // group_size
    pair_blocks = all_pairs.reshape(-1, BLK, head_local, 2 * HDIM)
    query_groups = seg_query.reshape(groups, group_size, BLK, head_local, HDIM)
    grad_groups = seg_grad.reshape(groups, group_size, BLK, head_local, HDIM)
    list_groups = block_lists.reshape(groups, group_size, KSEL)
    count_groups = block_counts.reshape(groups, group_size)
    empty = jnp.zeros(pair_blocks.shape, jnp.float32)

    def joint_turn(accum, operands):
        query_group, grad_group, list_group, count_group = operands
        gathered_key_blocks, gathered_value_blocks, usable = fetch_sets(
            pair_blocks, list_group, count_group
        )
        probability = probabilities(query_group, gathered_key_blocks, usable)
        reduced_precision = probability.astype(jnp.bfloat16)
        out_group = attend(reduced_precision, gathered_value_blocks)
        query_gradient, pair_terms = backward_group(
            gathered_key_blocks,
            gathered_value_blocks,
            query_group,
            grad_group,
            out_group,
            probability,
            reduced_precision,
        )
        return (accum.at[list_group].add(pair_terms), (out_group, query_gradient))

    accum, (out_groups, query_parts) = lax.scan(
        joint_turn, empty, (query_groups, grad_groups, list_groups, count_groups)
    )
    accum_rows = accum.reshape(-1, head_local, 2 * HDIM)
    summed = lax.psum_scatter(accum_rows, "blk", scatter_dimension=0, tiled=True)
    pair_grad = summed.astype(jnp.bfloat16)
    out_seg = out_groups.reshape(seg_rows, head_local, HDIM)
    query_seg = query_parts.reshape(seg_rows, head_local, HDIM)
    out_back, query_back, pair_back = (
        lax.all_to_all(out_seg, "uly", split_axis=0, concat_axis=1, tiled=True),
        lax.all_to_all(query_seg, "uly", split_axis=0, concat_axis=1, tiled=True),
        lax.all_to_all(pair_grad, "uly", split_axis=0, concat_axis=1, tiled=True),
    )
    return (
        out_back.reshape(tok_rows, width),
        query_back.reshape(tok_rows, width),
        pair_back[..., :HDIM].reshape(tok_rows, width),
        pair_back[..., HDIM:].reshape(tok_rows, width),
    )


def solution(mesh):
    placed = (
        P(("blk", "uly"), None),
        P(("blk", "uly"), None),
        P(("blk", "uly"), None),
        P(("blk", "uly"), None),
        P("blk", None),
        P("blk"),
    )
    return jax.shard_map(
        on_device,
        mesh=mesh,
        in_specs=placed,
        out_specs=(
            P(("blk", "uly"), None),
            P(("blk", "uly"), None),
            P(("blk", "uly"), None),
            P(("blk", "uly"), None),
        ),
        check_vma=False,
    )
```

profile of v0, /device:TPU:0, one launch (start us, length us, event | category | flops | bytes accessed | tf_op | source)
XLA Modules:
  0.0 136.0 jit_solution(9518933461510708066)
XLA Ops:
  7.2 1.0 copy.69
  8.2 1.0 copy.70
  9.3 16.0 %all_to_all.96 = bf16[128,8,128]{0,2,1:T(8,128)(2,1)S(1)} all-to-all(bf16[128,8,128]{0,2,1:T(8,128)(2,1)S(1)} %pad_maximum_fusion.1), channel_id=1, replica_groups=mesh['blk'=4,'uly'=8] {'uly'}, dimensions={1} | all-to-all | bytes 524288 | tf_op jit(solution)/shard_map/all_to_all | solution.py:86
  25.3 0.9 copy.71
  26.2 1.7 %copy.73 = bf16[128,512]{0,1:T(8,128)(2,1)} copy(bf16[128,512]{1,0:T(8,128)(2,1)} %param.6) | data formatting | bytes 262144 | tf_op args[0]
  27.8 3.6 %all-to-all-start.1 = ((bf16[128,8,64]{0,2,1:T(8,128)(2,1)}), bf16[128,8,64]{0,2,1:T(8,128)(2,1)S(1)}, u32[]{:S(2)}, u32[]{:S(2)}) async-start(bf16[128,8,64]{0,2,1:T(8,128)(2,1)} %bitcast.9), calls=%async_computation.1 | async-start | bytes 262144 | tf_op jit(solution)/shard_map/all_to_all | solution.py:85
  31.4 0.7 compare_select_fusion
  32.3 1.7 %copy.81 = bf16[128,512]{0,1:T(8,128)(2,1)} copy(bf16[128,512]{1,0:T(8,128)(2,1)} %param.9) | data formatting | bytes 262144 | tf_op args[3]
  34.0 4.8 %all-to-all-done.1 = bf16[128,8,64]{0,2,1:T(8,128)(2,1)S(1)} async-done(((bf16[128,8,64]{0,2,1:T(8,128)(2,1)}), bf16[128,8,64]{0,2,1:T(8,128)(2,1)S(1)}, u32[]{:S(2)}, u32[]{:S(2)}) %all-to-all-start.1) | async-done | bytes 131104 | tf_op jit(solution)/shard_map/all_to_all | solution.py:85
  38.8 3.4 %all-to-all-start.3 = ((bf16[128,8,64]{0,2,1:T(8,128)(2,1)}), bf16[128,8,64]{0,2,1:T(8,128)(2,1)S(1)}, u32[]{:S(2)}, u32[]{:S(2)}) async-start(bf16[128,8,64]{0,2,1:T(8,128)(2,1)} %bitcast.24), calls=%async_computation.3 | async-start | bytes 262144 | tf_op jit(solution)/shard_map/all_to_all | solution.py:87
  42.2 0.7 iota_compare_fusion
  43.1 6.3 %all-to-all-done.3 = bf16[128,8,64]{0,2,1:T(8,128)(2,1)S(1)} async-done(((bf16[128,8,64]{0,2,1:T(8,128)(2,1)}), bf16[128,8,64]{0,2,1:T(8,128)(2,1)S(1)}, u32[]{:S(2)}, u32[]{:S(2)}) %all-to-all-start.3) | async-done | bytes 131104 | tf_op jit(solution)/shard_map/all_to_all | solution.py:87
  50.0 2.2 %gather_fusion = bf16[128,64,128]{2,1,0:T(8,128)(2,1)S(1)} fusion(bf16[64,64,128]{2,1,0:T(8,128)(2,1)} %bitcast.208, s32[1024]{0:T(1024)S(1)} %pad_clamp_fusion), kind=kCustom, calls=%fused_computation | custom fusion | bytes 4194816 | tf_op jit(solution)/shard_map/while/body/eval_jaxpr/gather | solution.py:14
  52.2 1.0 fusion.1
  53.2 1.1 bitcast_reduce_fusion
  54.4 2.3 %fusion.33 = (f32[16,64]{1,0:T(8,128)S(1)}, bf16[16,64,1,64]{1,3,0,2:T(8,128)(2,1)S(1)}) fusion(f32[16,64,1,64]{1,0,3,2:T(8,128)S(1)} %reshape.172, f32[16,64]{1,0:T(8,128)S(1)} %bitcast_reduce_fusion, f32[16,64]{1,0:T(8,128)S(1)} %get-tuple-element.45, f32[16,8,64,64]{3,2,1,0:T(8,128)S(1)} %get-tuple-element.46, pred[16,8]{1,0:T(8,128)(4,1)S(1)} %iota_compare_fusion, ...), kind=kOutput, calls=%fused_computation.33 | convolution fusion | flops 69991424 | bytes 4599936 | tf_op jit(solution)/shard_map/while/body/eval_jaxpr/gqhjk,gjkhd->gqhd/dot_general | solution.py:29
  56.7 1.3 convolution_bitcast_fusion
  57.9 1.9 %fusion = bf16[16,64,1,8,64]{1,4,3,0,2:T(8,128)(2,1)S(1)} fusion(bf16[16,64,64,1]{2,1,3,0:T(8,128)(2,1)S(1)} %bitcast.231, f32[16,64]{1,0:T(8,128)S(1)} %get-tuple-element.47, f32[16,64]{1,0:T(8,128)S(1)} %bitcast_reduce_fusion, f32[16,64]{1,0:T(8,128)S(1)} %get-tuple-element.45, f32[16,8,64,64]{3,2,1,0:T(8,128)S(1)} %get-tuple-element.46, ...), kind=kOutput, calls=%fused_computation.4 | convolution fusion | flops 70778880 | bytes 5386368 | tf_op jit(solution)/shard_map/while/body/eval_jaxpr/gqhd,gjkhd->gqhjk/dot_general | solution.py:50
  59.8 0.7 multiply_bitcast_fusion
  60.5 3.1 %pad_maximum_fusion = f32[16,8,64,1,128]{4,2,1,0,3:T(8,128)} fusion(f32[16,8,64,1,64]{4,2,1,0,3:T(8,128)S(1)} %convolution_bitcast_fusion, f32[16,8,64,1,64]{4,2,1,0,3:T(8,128)S(1)} %multiply_bitcast_fusion), kind=kLoop, calls=%fused_computation.2 | loop fusion | flops 1048576 | bytes 8388608 | tf_op jit(solution)/shard_map/while/body/eval_jaxpr/concatenate | solution.py:72
  63.6 0.2 broadcast.65
  63.8 13.5 %scatter_fusion = f32[64,64,128]{2,1,0:T(8,128)S(1)} fusion(f32[64,64,128]{2,1,0:T(8,128)S(1)} %broadcast.65, s32[128]{0:T(128)S(1)} %reshape.177, f32[128,64,128]{2,1,0:T(8,128)} %bitcast.207), kind=kCustom, calls=%fused_computation.1 | custom fusion | flops 1048576 | bytes 12583424 | tf_op jit(solution)/shard_map/while/body/eval_jaxpr/scatter-add | solution.py:119
  77.4 1.3 copy-done
  79.1 0.5 broadcast.90
  79.6 2.3 %reduce.4 = bf16[1024,64]{1,0:T(8,128)(2,1)S(1)} reduce(bf16[1024,1,64]{2,1,0:T(2,128)(2,1)S(1)} %reshape.205, bf16[]{:T(256)} %broadcast.90), dimensions={1}, to_apply=%reshape.205.reduce_sub_computation | reduce | bytes 262146 | tf_op jit(solution)/shard_map/reshape | solution.py:127
  81.9 0.9 reshape.207
  82.8 3.6 %all-to-all-start.2 = ((bf16[8,2,4096]{2,1,0:T(2,128)(2,1)}), bf16[8,2,4096]{2,1,0:T(2,128)(2,1)S(1)}, u32[]{:S(2)}, u32[]{:S(2)}) async-start(bf16[8,2,4096]{2,1,0:T(2,128)(2,1)} %reshape.207), calls=%async_computation.2 | async-start | bytes 262144 | tf_op jit(solution)/shard_map/all_to_all | solution.py:130
  86.3 3.0 %fusion.27 = bf16[16,64,1,64]{1,3,0,2:T(8,128)(2,1)S(1)} fusion(bf16[16,64,1,8,64]{1,4,3,0,2:T(8,128)(2,1)} %copy-done.1, bf16[16,8,64,1,128]{4,2,1,0,3:T(8,128)(2,1)} %bitcast.213), kind=kOutput, calls=%fused_computation.30 | convolution fusion | flops 67239936 | bytes 3276800 | tf_op jit(solution)/shard_map/while/body/eval_jaxpr/gqhjk,gjkhd->gqhd/dot_general | solution.py:55
  89.4 0.2 copy.106
  89.7 2.3 %reduce.5 = bf16[1024,64]{1,0:T(8,128)(2,1)S(1)} reduce(bf16[1024,1,64]{2,1,0:T(2,128)(2,1)S(1)} %reshape.206, bf16[]{:T(256)} %broadcast.90), dimensions={1}, to_apply=%reshape.206.reduce_sub_computation | reduce | bytes 262146 | tf_op jit(solution)/shard_map/reshape | solution.py:128
  92.0 0.9 reshape.209
  92.9 0.5 all-to-all-done.2
  93.4 5.2 %all-to-all-start.4 = ((bf16[8,2,4096]{2,1,0:T(2,128)(2,1)}), bf16[8,2,4096]{2,1,0:T(2,128)(2,1)S(1)}, u32[]{:S(2)}, u32[]{:S(2)}) async-start(bf16[8,2,4096]{2,1,0:T(2,128)(2,1)} %reshape.209), calls=%async_computation.4 | async-start | bytes 262144 | tf_op jit(solution)/shard_map/all_to_all | solution.py:131
  98.7 9.4 %reduce-scatter.2.cloned.1.call-done = f32[1024,1,128]{2,1,0:T(1,128)} async-done(((f32[4096,1,128]{2,1,0:T(1,128)}), f32[1024,1,128]{2,1,0:T(1,128)}) %reduce-scatter.2.cloned.1.call-update) | async-done | bytes 524304 | tf_op jit(solution)/shard_map/reduce_scatter | solution.py:125
  108.1 1.4 %convert_element_type.61 = bf16[1024,1,128]{2,1,0:T(2,128)(2,1)S(1)} convert(f32[1024,1,128]{2,1,0:T(1,128)} %reduce-scatter.2.cloned.1.call-done) | non-fusion elementwise | flops 131072 | bytes 786432 | tf_op jit(solution)/shard_map/convert_element_type | solution.py:126
  109.5 2.2 %reduce.6 = bf16[1024,128]{1,0:T(8,128)(2,1)S(1)} reduce(bf16[1024,1,128]{2,1,0:T(2,128)(2,1)S(1)} %convert_element_type.61, bf16[]{:T(256)} %broadcast.90), dimensions={1}, to_apply=%convert_element_type.61.reduce_sub_computation | reduce | bytes 524290 | tf_op jit(solution)/shard_map/convert_element_type | solution.py:126
  111.7 0.8 reshape.211
  112.4 5.5 %all-to-all-start.5 = ((bf16[8,2,8192]{2,1,0:T(2,128)(2,1)}), bf16[8,2,8192]{2,1,0:T(2,128)(2,1)S(1)}, u32[]{:S(2)}, u32[]{:S(2)}) async-start(bf16[8,2,8192]{2,1,0:T(2,128)(2,1)} %reshape.211), calls=%async_computation.6 | async-start | bytes 524288 | tf_op jit(solution)/shard_map/all_to_all | solution.py:132
  118.0 0.3 reshape.208
  118.3 0.3 copy.79
  118.7 0.8 copy.93
  119.4 0.3 reshape.210
  119.8 0.3 copy.89
  120.1 0.8 copy.94
  120.9 6.0 %all-to-all-done.5 = bf16[8,2,8192]{2,1,0:T(2,128)(2,1)S(1)} async-done(((bf16[8,2,8192]{2,1,0:T(2,128)(2,1)}), bf16[8,2,8192]{2,1,0:T(2,128)(2,1)S(1)}, u32[]{:S(2)}, u32[]{:S(2)}) %all-to-all-start.5) | async-done | bytes 262176 | tf_op jit(solution)/shard_map/all_to_all | solution.py:132
  126.9 0.3 reshape.212
  127.5 0.8 copy.96
  128.4 0.8 copy.95
  (31 shorter events, 2.0 us)
Async XLA Ops:
  7.2 42.8 %all-gather.2.cloned.1.call-start = ((), (), s32[]{:S(2)}) async-start(), calls=%async_computation.7 | async-start | bytes 1310720 | tf_op jit(solution)/shard_map/all_gather | solution.py:89
  27.8 10.9 %all-to-all-start.1 = ((bf16[128,8,64]{0,2,1:T(8,128)(2,1)}), bf16[128,8,64]{0,2,1:T(8,128)(2,1)S(1)}, u32[]{:S(2)}, u32[]{:S(2)}) async-start(bf16[128,8,64]{0,2,1:T(8,128)(2,1)} %bitcast.9), calls=%async_computation.1 | async-start | bytes 262144 | tf_op jit(solution)/shard_map/all_to_all | solution.py:85
  38.8 10.7 %all-to-all-start.3 = ((bf16[128,8,64]{0,2,1:T(8,128)(2,1)}), bf16[128,8,64]{0,2,1:T(8,128)(2,1)S(1)}, u32[]{:S(2)}, u32[]{:S(2)}) async-start(bf16[128,8,64]{0,2,1:T(8,128)(2,1)} %bitcast.24), calls=%async_computation.3 | async-start | bytes 262144 | tf_op jit(solution)/shard_map/all_to_all | solution.py:87
  42.2 65.9 %reduce-scatter.2.cloned.1.call-start = ((), (), s32[]{:S(2)}) async-start(), calls=%async_computation.8 | async-start | bytes 2621440 | tf_op jit(solution)/shard_map/reduce_scatter | solution.py:125
  52.2 5.7 %copy-start.2 = (bf16[128,64,128]{2,1,0:T(8,128)(2,1)}, bf16[128,64,128]{2,1,0:T(8,128)(2,1)S(1)}, u32[]{:S(2)}) copy-start(bf16[128,64,128]{2,1,0:T(8,128)(2,1)S(1)} %gather_fusion) | copy-start | bytes 6291460
  59.8 3.8 %copy-start.1 = (bf16[16,64,1,8,64]{1,4,3,0,2:T(8,128)(2,1)}, bf16[16,64,1,8,64]{1,4,3,0,2:T(8,128)(2,1)S(1)}, u32[]{:S(2)}) copy-start(bf16[16,64,1,8,64]{1,4,3,0,2:T(8,128)(2,1)S(1)} %fusion) | copy-start | bytes 3145732
  77.4 1.4 copy-start
  82.8 10.7 %all-to-all-start.2 = ((bf16[8,2,4096]{2,1,0:T(2,128)(2,1)}), bf16[8,2,4096]{2,1,0:T(2,128)(2,1)S(1)}, u32[]{:S(2)}, u32[]{:S(2)}) async-start(bf16[8,2,4096]{2,1,0:T(2,128)(2,1)} %reshape.207), calls=%async_computation.2 | async-start | bytes 262144 | tf_op jit(solution)/shard_map/all_to_all | solution.py:130
  93.4 19.0 %all-to-all-start.4 = ((bf16[8,2,4096]{2,1,0:T(2,128)(2,1)}), bf16[8,2,4096]{2,1,0:T(2,128)(2,1)S(1)}, u32[]{:S(2)}, u32[]{:S(2)}) async-start(bf16[8,2,4096]{2,1,0:T(2,128)(2,1)} %reshape.209), calls=%async_computation.4 | async-start | bytes 262144 | tf_op jit(solution)/shard_map/all_to_all | solution.py:131
  112.4 14.4 %all-to-all-start.5 = ((bf16[8,2,8192]{2,1,0:T(2,128)(2,1)}), bf16[8,2,8192]{2,1,0:T(2,128)(2,1)S(1)}, u32[]{:S(2)}, u32[]{:S(2)}) async-start(bf16[8,2,8192]{2,1,0:T(2,128)(2,1)} %reshape.211), calls=%async_computation.6 | async-start | bytes 524288 | tf_op jit(solution)/shard_map/all_to_all | solution.py:132
Sparse Core Ops, SparseCore 0:
  26.3 15.7 all-gather.1
  78.9 29.1 reduce-scatter.1
where the time goes:
time: 137 us; the launch traced here: 136 us
  other arithmetic  27.4 us (20%)
  waiting for transfers between devices  27 us (20%)
  starting transfers between devices  21.3 us (16%)
  local copies, waits for them, and re-layouts  19.7 us (14%)
  blocking collectives  16 us (12%)
  between operations  14.4 us (11%)
  matrix products  10.2 us (7%)
    all_to_all x1, blocking collectives, on_device(): lax.all_to_all(pair_heads, 'uly', split_axis=1, concat_axis=0, tiled=True)  16 us
    scatter-add x1, other arithmetic, joint_turn(): return (accum.at[list_group].add(pair_terms), (out_group, query_gradient))  13.5 us
    unnamed x23, local copies, waits for them, and re-layouts  13.4 us
    reduce_scatter x1, waiting for transfers between devices, on_device(): lax.psum_scatter(accum_rows, 'blk', scatter_dimension=0, tiled=True)  9.4 us
    all_to_all x1, waiting for transfers between devices, on_device(): lax.all_to_all(grad_heads, 'uly', split_axis=1, concat_axis=0, tiled=True)  6.3 us
    all_to_all x1, waiting for transfers between devices, on_device(): lax.all_to_all(pair_grad, 'uly', split_axis=0, concat_axis=1, tiled=True)  5.97 us
    all_to_all x1, starting transfers between devices, on_device(): lax.all_to_all(pair_grad, 'uly', split_axis=0, concat_axis=1, tiled=True)  5.52 us
    all_to_all x1, starting transfers between devices, on_device(): lax.all_to_all(query_seg, 'uly', split_axis=0, concat_axis=1, tiled=True)  5.22 us
  transfers between devices with their start and end apart: 7, of which 5 were waited for; matrix products, arithmetic and copies ran while one was open for 17% of the time, Pallas kernels for 0%

commit v1 on v0

v1 whole, which is shorter than its diff:
```python
import functools
import math

import jax
import jax.numpy as jnp
from jax import lax
from jax.experimental import pallas as pl
from jax.experimental.pallas import tpu as pltpu
from jax.sharding import PartitionSpec as P

HDIM = 64
BLK = 64
KSEL = 8
PAIR = 2 * HDIM
SCALE = 1.0 / math.sqrt(HDIM)
VMEM_BYTES = 56 * 1024 * 1024


def dot(a, b, dims):
    return lax.dot_general(a, b, (dims, ((), ())), preferred_element_type=jnp.float32)


def attention_kernel(group, lists, counts, qd_ref, kv_ref, od_ref, dkv_ref, acc):
    local_blocks = qd_ref.shape[0] // BLK
    acc[...] = jnp.zeros_like(acc)
    first = lax.broadcasted_iota(jnp.int32, (BLK, PAIR), 1) < HDIM
    column = lax.broadcasted_iota(jnp.int32, (BLK, KSEL * BLK), 1)

    def one_block(b):
        rows = pl.ds(pl.multiple_of(b * BLK, BLK), BLK)
        picks = [pl.ds(pl.multiple_of(lists[b, j] * BLK, BLK), BLK) for j in range(KSEL)]
        qd = qd_ref[rows, :]
        zero = jnp.zeros_like(qd)
        diag = jnp.concatenate([jnp.where(first, qd, zero), jnp.where(first, zero, qd)], axis=0)
        kv = jnp.concatenate([kv_ref[pick, :] for pick in picks], axis=0)
        both = dot(diag, kv, ((1,), (1,)))
        scores = jnp.where(column < counts[b] * BLK, both[:BLK] * SCALE, -1e30)
        weights = jnp.exp(scores - jnp.max(scores, axis=1, keepdims=True))
        prob = weights * (1.0 / jnp.sum(weights, axis=1, keepdims=True))
        rounded = prob.astype(jnp.bfloat16)
        out = dot(rounded, kv, ((1,), (0,))).astype(jnp.bfloat16).astype(jnp.float32)
        delta = jnp.sum(jnp.where(first, 0.0, qd.astype(jnp.float32) * out), axis=1, keepdims=True)
        grad_score = (prob * (both[BLK:] - delta)).astype(jnp.bfloat16)
        dq = dot(grad_score, kv, ((1,), (0,))) * SCALE
        od_ref[rows, :] = jnp.where(first, dq, out).astype(jnp.bfloat16)
        terms = dot(jnp.concatenate([grad_score, rounded], axis=0), diag, ((0,), (0,)))
        return picks, terms

    def turn(g, carry):
        done = [one_block(g * group + i) for i in range(group)]
        for picks, terms in done:
            for j, pick in enumerate(picks):
                acc[pick, :] += terms[j * BLK : (j + 1) * BLK]
        return carry

    lax.fori_loop(0, local_blocks // group, turn, 0)
    lane = lax.broadcasted_iota(jnp.int32, (1, PAIR), 1)
    dkv_ref[...] = (acc[...] * jnp.where(lane < HDIM, SCALE, 1.0)).astype(dkv_ref.dtype)


def attention(block_lists, block_counts, qd, kv):
    heads_here, seg_rows, _ = qd.shape
    all_rows = kv.shape[1]

    def spec(rows):
        kind = {"pipeline_mode": pl.Buffered(1)} if heads_here > 1 else {}
        return pl.BlockSpec((None, rows, PAIR), lambda h, *_: (h, 0, 0), **kind)

    return pl.pallas_call(
        functools.partial(attention_kernel, math.gcd(2, seg_rows // BLK)),
        out_shape=(
            jax.ShapeDtypeStruct((heads_here, seg_rows, PAIR), jnp.bfloat16),
            jax.ShapeDtypeStruct((heads_here, all_rows, PAIR), jnp.bfloat16),
        ),
        grid_spec=pltpu.PrefetchScalarGridSpec(
            num_scalar_prefetch=2,
            grid=(heads_here,),
            in_specs=[spec(seg_rows), spec(all_rows)],
            out_specs=[spec(seg_rows), spec(all_rows)],
            scratch_shapes=[pltpu.VMEM((all_rows, PAIR), jnp.float32)],
        ),
        compiler_params=pltpu.CompilerParams(vmem_limit_bytes=VMEM_BYTES),
        name="attention",
    )(block_lists, block_counts, qd, kv)


def on_device(query_rows, key_rows, value_rows, out_grad, block_lists, block_counts):
    rows, width = query_rows.shape
    heads = width // HDIM

    def by_head(array):
        return array.reshape(rows, heads, HDIM)

    packed = jnp.concatenate([by_head(a) for a in (query_rows, out_grad, key_rows, value_rows)], axis=2)
    packed = packed.transpose(1, 0, 2)
    seg = lax.all_to_all(packed, "uly", split_axis=0, concat_axis=1, tiled=True)
    qd = seg[..., :PAIR]
    kv = lax.all_gather(seg[..., PAIR:], "blk", axis=1, tiled=True)
    od, dkv = attention(block_lists, block_counts, qd, kv)
    dkv = lax.psum_scatter(dkv.astype(jnp.float32), "blk", scatter_dimension=1, tiled=True)
    both = jnp.concatenate([od, dkv.astype(jnp.bfloat16)], axis=2)
    back = lax.all_to_all(both, "uly", split_axis=1, concat_axis=0, tiled=True)
    back = back.transpose(1, 0, 2).reshape(rows, heads, 4, HDIM)
    dq, out, dk, dv = (back[:, :, i].reshape(rows, width) for i in range(4))
    return out, dq, dk, dv


def solution(mesh):
    tokens = P(("blk", "uly"), None)
    return jax.shard_map(
        on_device,
        mesh=mesh,
        in_specs=(tokens, tokens, tokens, tokens, P("blk", None), P("blk")),
        out_specs=(tokens, tokens, tokens, tokens),
        check_vma=False,
    )
```

time: 137 us -> 126 us (0.920)
  blocking collectives: 16 us -> 41.5 us
  other arithmetic: 27.4 us -> 4.87 us
  starting transfers between devices: 21.3 us -> 0.08 us
  Pallas kernels: 0 us -> 15.1 us
  waiting for transfers between devices: 27 us -> 39.6 us
  matrix products: 10.2 us -> 0 us
  local copies, waits for them, and re-layouts: 19.7 us -> 10.7 us
    all_to_all x1 -> x2, blocking collectives: 16 us -> 41.5 us  [the longest x1 21.6 us: on_device(): seg = lax.all_to_all(packed, 'uly', split_axis=0, concat_axis=1, tiled=True)]
    all_to_all x5 -> x0, starting transfers between devices: 21.3 us -> none  [the longest x1 5.52 us: on_device(): lax.all_to_all(pair_grad, 'uly', split_axis=0, concat_axis=1, tiled=True)]
    all_to_all x5 -> x0, waiting for transfers between devices: 17.6 us -> none  [the longest x1 6.3 us: on_device(): lax.all_to_all(grad_heads, 'uly', split_axis=1, concat_axis=0, tiled=True)]
    reduce_scatter x1, waiting for transfers between devices: 9.4 us -> 25 us  [on_device(): lax.psum_scatter(dkv.astype(jnp.float32), 'blk', scatter_dimension=1, til...]
    pallas_call x0 -> x1, Pallas kernels: none -> 15.1 us  [attention(): pl.pallas_call(functools.partial(attention_kernel, math.gcd(2, seg_rows /...]
    all_gather x1, waiting for transfers between devices: 0.02 us -> 14.6 us  [on_device(): kv = lax.all_gather(seg[..., PAIR:], 'blk', axis=1, tiled=True)]
    scatter-add x1 -> x0, other arithmetic: 13.5 us -> none  [joint_turn(): return (accum.at[list_group].add(pair_terms), (out_group, query_gradient))]
    dot_general x6 -> x0, matrix products: 10.2 us -> none  [the longest x1 3.04 us: backward_group(): jnp.einsum('gqhjk,gjkhd->gqhd', score_gradient, gathered_key_blocks, pref...]
  transfers between devices with their start and end apart: 7 -> 2, of which waited for: 5 -> 2; matrix products, arithmetic and copies ran while one was open for 17% -> 1% of each run, Pallas kernels for 0% -> 0%
where the time goes in v1:
time: 126 us
  blocking collectives  41.5 us (33%)
  waiting for transfers between devices  39.6 us (31%)
  Pallas kernels  15.1 us (12%)
  between operations  14.2 us (11%)
  local copies, waits for them, and re-layouts  10.7 us (8%)
  other arithmetic  4.87 us (4%)
    reduce_scatter x1, waiting for transfers between devices, on_device(): lax.psum_scatter(dkv.astype(jnp.float32), 'blk', scatter_dimension=1, til...  25 us
    all_to_all x1, blocking collectives, on_device(): seg = lax.all_to_all(packed, 'uly', split_axis=0, concat_axis=1, tiled=True)  21.6 us
    all_to_all x1, blocking collectives, on_device(): back = lax.all_to_all(both, 'uly', split_axis=1, concat_axis=0, tiled=True)  19.8 us
    pallas_call x1, Pallas kernels, attention(): pl.pallas_call(functools.partial(attention_kernel, math.gcd(2, seg_rows /...  15.1 us
    all_gather x1, waiting for transfers between devices, on_device(): kv = lax.all_gather(seg[..., PAIR:], 'blk', axis=1, tiled=True)  14.6 us
    unnamed x23, local copies, waits for them, and re-layouts  8.57 us
    unnamed x1, other arithmetic  3.82 us
  transfers between devices with their start and end apart: 2, of which 2 were waited for; matrix products, arithmetic and copies ran while one was open for 1% of the time, Pallas kernels for 0%

profile of v1, /device:TPU:0, one launch (start us, length us, event | category | flops | bytes accessed | tf_op | source)
XLA Modules:
  0.0 126.0 jit_solution(11367028398789224228)
XLA Ops:
  7.2 0.0 copy-start.1
  7.2 0.0 all-gather.2.cloned.1.call-start
  7.2 1.1 copy.41
  8.3 0.0 copy-done.1
  8.3 0.0 copy-start.2
  8.3 0.1 copy.42
  8.4 0.8 copy-done.2
  9.2 0.0 copy-start.3
  9.2 0.1 copy.43
  9.3 0.8 copy-done.3
  10.1 0.1 copy.44
  10.3 21.6 %all_to_all.24 = bf16[8,128,256]{1,2,0:T(8,128)(2,1)S(1)} all-to-all(bf16[8,128,256]{1,2,0:T(8,128)(2,1)S(1)} %maximum_bitcast_fusion), channel_id=1, replica_groups=mesh['blk'=4,'uly'=8] {'uly'}, dimensions={0} | all-to-all | bytes 1048576 | tf_op jit(solution)/shard_map/all_to_all | solution.py:96
  31.9 0.2 copy.45
  32.1 0.8 fusion.1
  32.9 0.0 copy-start.4
  32.9 0.0 all-gather.2.cloned.1.call-update
  33.0 0.0 reduce-scatter.2.cloned.1.call-start
  33.0 0.6 copy-done.4
  33.6 0.7 copy.46.lists
  34.3 14.6 %all-gather.2.cloned.1.call-done.kv_ref = bf16[1,4096,128]{2,1,0:T(8,128)(2,1)} async-done(((bf16[1,1024,128]{2,1,0:T(8,128)(2,1)}), bf16[1,4096,128]{2,1,0:T(8,128)(2,1)}) %all-gather.2.cloned.1.call-update) | async-done | bytes 1048592 | tf_op jit(solution)/shard_map/all_gather | solution.py:98
  48.9 15.1 %attention.1 = (bf16[1,1024,128]{2,1,0:T(8,128)(2,1)}, bf16[1,4096,128]{2,1,0:T(8,128)(2,1)}) custom-call(s32[16,8]{1,0:T(8,128)} %copy.46.lists, s32[16]{0:T(128)} %counts.1, bf16[1,1024,128]{2,1,0:T(8,128)(2,1)} %get-tuple-element.25.qd_ref, bf16[1,4096,128]{2,1,0:T(8,128)(2,1)} %all-gather.2.cloned.1.call-done.kv_ref), custom_call_target="tpu_custom_call" | custom-call | tf_op jit(solution)/shard_map/attention/pallas_call | solution.py:69
  63.9 0.0 copy-start
  63.9 0.0 reduce-scatter.2.cloned.1.call-update
  64.0 25.0 %reduce-scatter.2.cloned.1.call-done = bf16[1,1024,128]{2,1,0:T(8,128)(2,1)} async-done(((bf16[1,4096,128]{2,1,0:T(8,128)(2,1)}), bf16[1,1024,128]{2,1,0:T(8,128)(2,1)}) %reduce-scatter.2.cloned.1.call-update) | async-done | bytes 262160 | tf_op jit(solution)/shard_map/reduce_scatter | solution.py:100
  89.0 0.0 copy-done
  89.0 1.0 pad_maximum_fusion
  90.0 0.8 copy.55
  90.8 0.5 broadcast
  91.4 3.8 %reduce = bf16[1024,256]{1,0:T(8,128)(2,1)S(1)} reduce(bf16[1024,1,256]{2,1,0:T(2,128)(2,1)S(1)} %bitcast.20, bf16[]{:T(256)} %broadcast), dimensions={1}, to_apply=%bitcast.18.reduce_sub_computation | reduce | bytes 1048578
  95.2 0.1 reshape.34
  95.3 19.8 %all_to_all.25 = bf16[8,2,16384]{2,1,0:T(2,128)(2,1)S(1)} all-to-all(bf16[8,2,16384]{2,1,0:T(2,128)(2,1)S(1)} %reshape.34), channel_id=1, replica_groups=mesh['blk'=4,'uly'=8] {'uly'}, dimensions={0} | all-to-all | bytes 1048576 | tf_op jit(solution)/shard_map/all_to_all | solution.py:102
  115.2 0.5 reshape.35
  115.7 0.1 copy.53
  115.8 0.3 copy.48
  116.1 0.8 copy.49
  116.9 0.8 copy.50
  117.6 0.8 copy.51
  118.4 0.8 copy.52
  (2 shorter events, 0.1 us)
Async XLA Ops:
  7.2 1.1 copy-start.1
  7.2 41.7 %all-gather.2.cloned.1.call-start = ((), (), s32[]{:S(2)}) async-start(), calls=%async_computation.3 | async-start | bytes 1310720 | tf_op jit(solution)/shard_map/all_gather | solution.py:98
  8.3 0.9 copy-start.2
  9.2 0.9 copy-start.3
  32.9 0.7 copy-start.4
  33.0 56.0 %reduce-scatter.2.cloned.1.call-start = ((), (), s32[]{:S(2)}) async-start(), calls=%async_computation.4 | async-start | bytes 1310720 | tf_op jit(solution)/shard_map/reduce_scatter | solution.py:100
  63.9 25.1 %copy-start = (bf16[1,1024,128]{2,1,0:T(8,128)(2,1)S(1)}, bf16[1,1024,128]{2,1,0:T(8,128)(2,1)}, u32[]{:S(2)}) copy-start(bf16[1,1024,128]{2,1,0:T(8,128)(2,1)} %get-tuple-element.6) | copy-start | bytes 786436
Sparse Core Ops, SparseCore 0:
  33.1 15.7 all-gather.1
  64.1 24.8 reduce-scatter.1

commit v2 on v1

--- a/solution.py
+++ b/solution.py
@@ -84,31 +84,267 @@
     )(block_lists, block_counts, qd, kv)
 
 
-def on_device(query_rows, key_rows, value_rows, out_grad, block_lists, block_counts):
+MESH = pl.DeviceIdType.MESH
+
+
+def places():
+    seg, lane = lax.axis_index("blk"), lax.axis_index("uly")
+    core = lax.rem(seg, 2)
+    return seg, lane, seg + 1 - 2 * core, lax.rem(seg + 2, 4)
+
+
+def remote(src, dst, send, recv, device):
+    return pltpu.make_async_remote_copy(
+        src_ref=src, dst_ref=dst, send_sem=send, recv_sem=recv, device_id=device, device_id_type=MESH
+    )
+
+
+def greet(lanes):
+    seg, lane, other, across = places()
+    barrier = pltpu.get_barrier_semaphore()
+
+    def one(i, carry):
+        device = (seg, lax.rem(lane + i, lanes))
+        pl.semaphore_signal(barrier, inc=1, device_id=device, device_id_type=MESH)
+        return carry
+
+    lax.fori_loop(1, lanes, one, 0)
+    for near in (other, across):
+        pl.semaphore_signal(barrier, inc=1, device_id=(near, lane), device_id_type=MESH)
+    return barrier
+
+
+def loop(start, stop, body):
+    lax.fori_loop(start, stop, lambda i, carry: (body(i), carry)[1], 0)
+
+
+def join(left, right):
+    return jnp.concatenate([left, right], axis=1)
+
+
+def gather_kernel(
+    lanes, q_ref, k_ref, v_ref, g_ref, qd, kv, qd_out, kv_out, qd_s, qd_r, kv_s, kv_r, x_s, x_r, c_s, c_r
+):
+    seg, lane, other, across = places()
+    heads_here = qd.shape[1]
+    barrier = greet(lanes)
+
+    def pack(left, right, to):
+        for h in range(lanes * heads_here):
+            columns = slice(h * HDIM, (h + 1) * HDIM)
+            to[h // heads_here, h % heads_here] = join(left[:, columns], right[:, columns])
+
+    pack(k_ref, v_ref, kv_out)
+    pl.semaphore_wait(barrier, lanes + 1)
+
+    def kv_copy(i, target, source):
+        return remote(kv_out.at[target], kv.at[seg, source], kv_s.at[i], kv_r.at[i], (seg, target))
+
+    def qd_copy(i, target, source):
+        return remote(qd_out.at[target], qd.at[source], qd_s.at[i], qd_r.at[i], (seg, target))
+
+    def x_copy(i, source, whose):
+        return remote(kv.at[whose, source], kv.at[whose, source], x_s.at[i], x_r.at[i], (across, lane))
+
+    def c_copy(n, i, source, whose):
+        block = kv.at[whose, source]
+        return remote(block, block, c_s.at[n, i], c_r.at[n, i], (other, lane))
+
+    def ahead(i):
+        return lax.rem(lane + i, lanes)
+
+    def behind(i):
+        return lax.rem(lane + lanes - i, lanes)
+
+    loop(1, lanes, lambda i: kv_copy(i, ahead(i), lane).start())
+    kv[seg, lane] = kv_out[lane]
+    x_copy(0, lane, seg).start()
+    c_copy(0, 0, lane, seg).start()
+    pack(q_ref, g_ref, qd_out)
+    loop(1, lanes, lambda i: qd_copy(i, ahead(i), lane).start())
+    qd[lane] = qd_out[lane]
+
+    def relay(i):
+        x_copy(i, behind(i), across).wait_recv()
+        c_copy(1, i, behind(i), across).start()
+
+    def arrive(i):
+        kv_copy(i, lane, behind(i)).wait_recv()
+        x_copy(i, behind(i), seg).start()
+        c_copy(0, i, behind(i), seg).start()
+        relay(i - 1)
+
+    loop(1, lanes, arrive)
+    relay(lanes - 1)
+
+    def finish(i):
+        c_copy(0, i, behind(i), other).wait_recv()
+        c_copy(1, i, behind(i), lax.rem(other + 2, 4)).wait_recv()
+        x_copy(i, behind(i), seg).wait_send()
+        c_copy(0, i, behind(i), seg).wait_send()
+        c_copy(1, i, behind(i), across).wait_send()
+
+    loop(0, lanes, finish)
+
+    def finish_lanes(i):
+        qd_copy(i, lane, behind(i)).wait_recv()
+        qd_copy(i, ahead(i), lane).wait_send()
+        kv_copy(i, ahead(i), lane).wait_send()
+
+    loop(1, lanes, finish_lanes)
+
+
+def return_kernel(
+    lanes, od, dkv, out_ref, dq_ref, dk_ref, dv_ref,
+    od_in, core_in, x_out, x_in, end_out, end_in,
+    od_s, od_r, c_s, c_r, x_s, x_r, e_s, e_r,
+):
+    seg, lane, other, across = places()
+    heads_here = od.shape[1]
+    barrier = greet(lanes)
+
+    def ahead(i):
+        return lax.rem(lane + i, lanes)
+
+    def behind(i):
+        return lax.rem(lane + lanes - i, lanes)
+
+    def od_copy(i, target, source):
+        return remote(od.at[target], od_in.at[source], od_s.at[i], od_r.at[i], (seg, target))
+
+    def end_copy(i, target, source):
+        return remote(end_out.at[target], end_in.at[source], e_s.at[i], e_r.at[i], (seg, target))
+
+    def c_copy(n, i, whose):
+        return remote(dkv.at[whose, ahead(i)], core_in.at[n, ahead(i)], c_s.at[n, i], c_r.at[n, i], (other, lane))
+
+    def x_copy(i):
+        return remote(x_out.at[ahead(i)], x_in.at[ahead(i)], x_s.at[i], x_r.at[i], (across, lane))
+
+    def send(i):
+        c_copy(1, i, lax.rem(other + 2, 4)).start()
+        c_copy(0, i, other).start()
+
+    def wide(block):
+        return block.astype(jnp.float32)
+
+    def reduce_core(i):
+        c_copy(1, i, other).wait_recv()
+        to = ahead(i)
+        x_out[to] = (wide(dkv[across, to]) + wide(core_in[1, to])).astype(jnp.bfloat16)
+        x_copy(i).start()
+
+    def total(i):
+        c_copy(0, i, other).wait_recv()
+        x_copy(i).wait_recv()
+        to = ahead(i)
+        return (wide(dkv[seg, to]) + wide(core_in[0, to]) + wide(x_in[to])).astype(jnp.bfloat16)
+
+    def reduce_chip(i):
+        end_out[ahead(i)] = total(i)
+        end_copy(i, ahead(i), lane).start()
+
+    lag = min(2, lanes - 1)
+    pl.semaphore_wait(barrier, lanes + 1)
+    loop(1, lanes + 1, send)
+    loop(1, lanes, lambda i: od_copy(i, ahead(i), lane).start())
+    od_in[lane] = od[lane]
+    loop(1, lag + 1, reduce_core)
+
+    def both(i):
+        reduce_core(i)
+        reduce_chip(i - lag)
+
+    loop(lag + 1, lanes + 1, both)
+    loop(lanes + 1 - lag, lanes, reduce_chip)
+    end_in[lane] = total(lanes)
+
+    def unpack(block, left, right):
+        for h in range(0, lanes * heads_here, 2):
+            a, b = (block[g // heads_here, g % heads_here] for g in (h, h + 1))
+            columns = slice(h * HDIM, (h + 2) * HDIM)
+            left[:, columns] = join(a[:, :HDIM], b[:, :HDIM])
+            right[:, columns] = join(a[:, HDIM:], b[:, HDIM:])
+
+    loop(1, lanes, lambda i: od_copy(i, lane, behind(i)).wait_recv())
+    unpack(od_in, dq_ref, out_ref)
+    loop(1, lanes, lambda i: end_copy(i, lane, behind(i)).wait_recv())
+    unpack(end_in, dk_ref, dv_ref)
+
+    def finish(i):
+        c_copy(0, i, other).wait_send()
+        c_copy(1, i, other).wait_send()
+        x_copy(i).wait_send()
+
+    loop(1, lanes + 1, finish)
+
+    def finish_lanes(i):
+        od_copy(i, ahead(i), lane).wait_send()
+        end_copy(i, ahead(i), lane).wait_send()
+
+    loop(1, lanes, finish_lanes)
+
+
+def comm_params(number):
+    return pltpu.CompilerParams(
+        collective_id=number, has_side_effects=True, vmem_limit_bytes=VMEM_BYTES
+    )
+
+
+def on_device(lanes, query_rows, key_rows, value_rows, out_grad, block_lists, block_counts):
     rows, width = query_rows.shape
-    heads = width // HDIM
-
-    def by_head(array):
-        return array.reshape(rows, heads, HDIM)
-
-    packed = jnp.concatenate([by_head(a) for a in (query_rows, out_grad, key_rows, value_rows)], axis=2)
-    packed = packed.transpose(1, 0, 2)
-    seg = lax.all_to_all(packed, "uly", split_axis=0, concat_axis=1, tiled=True)
-    qd = seg[..., :PAIR]
-    kv = lax.all_gather(seg[..., PAIR:], "blk", axis=1, tiled=True)
+    heads_here = width // HDIM // lanes
+    segs = 4
+    block = (heads_here, rows, PAIR)
+    vmem = pl.BlockSpec(memory_space=pltpu.VMEM)
+    dma = pltpu.SemaphoreType.DMA
+    half = jnp.bfloat16
+
+    qd, kv = pl.pallas_call(
+        functools.partial(gather_kernel, lanes),
+        out_shape=(
+            jax.ShapeDtypeStruct((lanes, *block), half),
+            jax.ShapeDtypeStruct((segs, lanes, *block), half),
+        ),
+        in_specs=[vmem] * 4,
+        out_specs=(vmem, vmem),
+        scratch_shapes=[pltpu.VMEM((lanes, *block), half)] * 2
+        + [dma((lanes,))] * 6
+        + [dma((2, lanes))] * 2,
+        compiler_params=comm_params(0),
+        name="gather",
+    )(query_rows, key_rows, value_rows, out_grad)
+
+    qd = qd.transpose(1, 0, 2, 3).reshape(heads_here, lanes * rows, PAIR)
+    kv = kv.transpose(2, 0, 1, 3, 4).reshape(heads_here, segs * lanes * rows, PAIR)
     od, dkv = attention(block_lists, block_counts, qd, kv)
-    dkv = lax.psum_scatter(dkv.astype(jnp.float32), "blk", scatter_dimension=1, tiled=True)
-    both = jnp.concatenate([od, dkv.astype(jnp.bfloat16)], axis=2)
-    back = lax.all_to_all(both, "uly", split_axis=1, concat_axis=0, tiled=True)
-    back = back.transpose(1, 0, 2).reshape(rows, heads, 4, HDIM)
-    dq, out, dk, dv = (back[:, :, i].reshape(rows, width) for i in range(4))
-    return out, dq, dk, dv
+    od = od.reshape(heads_here, lanes, rows, PAIR).transpose(1, 0, 2, 3)
+    dkv = dkv.reshape(heads_here, segs, lanes, rows, PAIR).transpose(1, 2, 0, 3, 4)
+
+    return tuple(
+        pl.pallas_call(
+            functools.partial(return_kernel, lanes),
+            out_shape=[jax.ShapeDtypeStruct((rows, width), half)] * 4,
+            in_specs=[vmem] * 2,
+            out_specs=[vmem] * 4,
+            scratch_shapes=[
+                pltpu.VMEM((lanes, *block), half),
+                pltpu.VMEM((2, lanes, *block), half),
+            ]
+            + [pltpu.VMEM((lanes, *block), half)] * 4
+            + [dma((lanes + 1,))] * 2
+            + [dma((2, lanes + 1))] * 2
+            + [dma((lanes + 1,))] * 4,
+            compiler_params=comm_params(1),
+            name="scatter",
+        )(od, dkv)
+    )
 
 
 def solution(mesh):
     tokens = P(("blk", "uly"), None)
     return jax.shard_map(
-        on_device,
+        functools.partial(on_device, mesh.shape["uly"]),
         mesh=mesh,
         in_specs=(tokens, tokens, tokens, tokens, P("blk", None), P("blk")),
         out_specs=(tokens, tokens, tokens, tokens),

time: 126 us -> 67 us (0.53)
  Pallas kernels: 15.1 us -> 60.5 us
  blocking collectives: 41.5 us -> 0 us
  waiting for transfers between devices: 39.6 us -> 0 us
  between operations: 14.2 us -> 0.66 us
  local copies, waits for them, and re-layouts: 10.7 us -> 5.52 us
  other arithmetic: 4.87 us -> 0 us
    pallas_call x0 -> x2, Pallas kernels: none -> 45.5 us  [the longest x1 25.6 us: on_device(): pl.pallas_call(functools.partial(gather_kernel, lanes), out_shape=(jax.Sh...]
    all_to_all x2 -> x0, blocking collectives: 41.5 us -> none  [the longest x1 21.6 us: on_device(): seg = lax.all_to_all(packed, 'uly', split_axis=0, concat_axis=1, tiled=True)]
    reduce_scatter x1 -> x0, waiting for transfers between devices: 25 us -> none  [on_device(): lax.psum_scatter(dkv.astype(jnp.float32), 'blk', scatter_dimension=1, til...]
    all_gather x1 -> x0, waiting for transfers between devices: 14.6 us -> none  [on_device(): kv = lax.all_gather(seg[..., PAIR:], 'blk', axis=1, tiled=True)]
    unnamed x1 -> x0, other arithmetic: 3.82 us -> none
    unnamed x23 -> x11, local copies, waits for them, and re-layouts: 8.57 us -> 5.52 us
  transfers between devices with their start and end apart: 2 -> 0, of which waited for: 2 -> 0; matrix products, arithmetic and copies ran while one was open for 1% -> 0% of each run, Pallas kernels for 0% -> 0%
where the time goes in v2:
time: 67 us; the launch traced here: 66.7 us
  Pallas kernels  60.5 us (90%)
  local copies, waits for them, and re-layouts  5.52 us (8%)
    pallas_call x1, Pallas kernels, on_device(): pl.pallas_call(functools.partial(gather_kernel, lanes), out_shape=(jax.Sh...  25.6 us
    pallas_call x1, Pallas kernels, on_device(): pl.pallas_call(functools.partial(return_kernel, lanes), out_shape=[jax.Sh...  19.9 us
    pallas_call x1, Pallas kernels, attention(): pl.pallas_call(functools.partial(attention_kernel, math.gcd(2, seg_rows /...  15 us
    unnamed x11, local copies, waits for them, and re-layouts  5.52 us

profile of v2, /device:TPU:0, one launch (start us, length us, event | category | flops | bytes accessed | tf_op | source)
XLA Modules:
  0.0 66.7 jit_solution(13428613429902384977)
XLA Ops:
  0.6 1.4 %copy.10.lists = s32[16,8]{1,0:T(8,128)} copy(s32[16,8]{0,1:T(8,128)} %param.10) | data formatting | bytes 1024 | tf_op args[4]
  2.0 25.6 %gather.1 = (bf16[8,1,128,128]{3,2,1,0:T(8,128)(2,1)}, bf16[4,8,1,128,128]{4,3,2,1,0:T(8,128)(2,1)}) custom-call(bf16[128,512]{1,0:T(8,128)(2,1)} %q_ref.1, bf16[128,512]{1,0:T(8,128)(2,1)} %k_ref.1, bf16[128,512]{1,0:T(8,128)(2,1)} %v_ref.1, bf16[128,512]{1,0:T(8,128)(2,1)} %g_ref.1), custom_call_target="tpu_custom_call" | custom-call | tf_op jit(solution)/shard_map/gather/pallas_call | solution.py:303
  27.6 15.0 %attention.1 = (bf16[1,1024,128]{2,1,0:T(8,128)(2,1)}, bf16[1,4096,128]{2,1,0:T(8,128)(2,1)}) custom-call(s32[16,8]{1,0:T(8,128)} %copy.10.lists, s32[16]{0:T(128)} %counts.1, bf16[1,1024,128]{2,1,0:T(8,128)(2,1)} %bitcast.7, bf16[1,4096,128]{2,1,0:T(8,128)(2,1)} %bitcast.5), custom_call_target="tpu_custom_call" | custom-call | tf_op jit(solution)/shard_map/attention/pallas_call | solution.py:69
  42.6 19.9 %scatter.1 = (bf16[128,512]{1,0:T(8,128)(2,1)}, bf16[128,512]{1,0:T(8,128)(2,1)}, bf16[128,512]{1,0:T(8,128)(2,1)}, bf16[128,512]{1,0:T(8,128)(2,1)}) custom-call(bf16[8,1,128,128]{3,2,1,0:T(8,128)(2,1)} %bitcast.6, bf16[4,8,1,128,128]{4,3,2,1,0:T(8,128)(2,1)} %bitcast.4), custom_call_target="tpu_custom_call" | custom-call | tf_op jit(solution)/shard_map/scatter/pallas_call | solution.py:325
  62.5 0.0 copy-start.2
  62.5 1.6 %copy.15 = bf16[128,512]{1,0:T(8,128)(2,1)} copy(bf16[128,512]{1,0:T(8,128)(2,1)} %get-tuple-element.16) | data formatting | bytes 262144
  64.1 0.0 copy-done.2
  64.1 0.0 copy-start.1
  64.1 0.7 copy.16
  64.8 0.3 copy-done.1
  65.1 0.0 copy-start
  65.1 0.7 copy.17
  65.7 0.3 copy-done
  66.0 0.7 copy.18
Async XLA Ops:
  62.5 1.6 %copy-start.2 = (bf16[128,512]{1,0:T(8,128)(2,1)S(1)}, bf16[128,512]{1,0:T(8,128)(2,1)}, u32[]{:S(2)}) copy-start(bf16[128,512]{1,0:T(8,128)(2,1)} %get-tuple-element.17) | copy-start | bytes 393220
  64.1 1.0 %copy-start.1 = (bf16[128,512]{1,0:T(8,128)(2,1)S(1)}, bf16[128,512]{1,0:T(8,128)(2,1)}, u32[]{:S(2)}) copy-start(bf16[128,512]{1,0:T(8,128)(2,1)} %get-tuple-element.18) | copy-start | bytes 393220
  65.1 1.0 %copy-start = (bf16[128,512]{1,0:T(8,128)(2,1)S(1)}, bf16[128,512]{1,0:T(8,128)(2,1)}, u32[]{:S(2)}) copy-start(bf16[128,512]{1,0:T(8,128)(2,1)} %get-tuple-element.19) | copy-start | bytes 393220

commit v3 on v2

--- a/solution.py
+++ b/solution.py
@@ -13,37 +13,54 @@
 KSEL = 8
 PAIR = 2 * HDIM
 SCALE = 1.0 / math.sqrt(HDIM)
-VMEM_BYTES = 56 * 1024 * 1024
+GROUP = 8
+MIB = 1024 * 1024
 
 
 def dot(a, b, dims):
     return lax.dot_general(a, b, (dims, ((), ())), preferred_element_type=jnp.float32)
 
 
-def attention_kernel(group, lists, counts, qd_ref, kv_ref, od_ref, dkv_ref, acc):
+def attention_kernel(group, lists_hbm, counts_hbm, qd, kv, od, dkv, lists, counts, acc, sems):
+    loads = (
+        pltpu.make_async_copy(lists_hbm, lists, sems.at[0]),
+        pltpu.make_async_copy(counts_hbm, counts, sems.at[1]),
+    )
+    for load in loads:
+        load.start()
+    for h in range(qd.shape[0]):
+        acc[...] = jnp.zeros_like(acc)
+        if h == 0:
+            for load in loads:
+                load.wait()
+        attend_head(group, lists, counts, qd.at[h], kv.at[h], od.at[h], acc)
+        dkv[h] = acc[...].astype(dkv.dtype)
+
+
+def attend_head(group, lists, counts, qd_ref, kv_ref, od_ref, acc):
     local_blocks = qd_ref.shape[0] // BLK
-    acc[...] = jnp.zeros_like(acc)
-    first = lax.broadcasted_iota(jnp.int32, (BLK, PAIR), 1) < HDIM
+    lane = lax.broadcasted_iota(jnp.int32, (BLK, PAIR), 1)
+    first = lane < HDIM
     column = lax.broadcasted_iota(jnp.int32, (BLK, KSEL * BLK), 1)
 
     def one_block(b):
         rows = pl.ds(pl.multiple_of(b * BLK, BLK), BLK)
-        picks = [pl.ds(pl.multiple_of(lists[b, j] * BLK, BLK), BLK) for j in range(KSEL)]
+        picks = [pl.ds(pl.multiple_of(lists[j, b] * BLK, BLK), BLK) for j in range(KSEL)]
         qd = qd_ref[rows, :]
         zero = jnp.zeros_like(qd)
-        diag = jnp.concatenate([jnp.where(first, qd, zero), jnp.where(first, zero, qd)], axis=0)
+        diag = jnp.concatenate([jnp.where(first, qd * SCALE, zero), jnp.where(first, zero, qd)], axis=0)
         kv = jnp.concatenate([kv_ref[pick, :] for pick in picks], axis=0)
         both = dot(diag, kv, ((1,), (1,)))
-        scores = jnp.where(column < counts[b] * BLK, both[:BLK] * SCALE, -1e30)
+        scores = jnp.where(column < counts[b] * BLK, both[:BLK], -1e30)
         weights = jnp.exp(scores - jnp.max(scores, axis=1, keepdims=True))
         prob = weights * (1.0 / jnp.sum(weights, axis=1, keepdims=True))
         rounded = prob.astype(jnp.bfloat16)
-        out = dot(rounded, kv, ((1,), (0,))).astype(jnp.bfloat16).astype(jnp.float32)
-        delta = jnp.sum(jnp.where(first, 0.0, qd.astype(jnp.float32) * out), axis=1, keepdims=True)
+        delta = jnp.sum(rounded.astype(jnp.float32) * both[BLK:], axis=1, keepdims=True)
         grad_score = (prob * (both[BLK:] - delta)).astype(jnp.bfloat16)
-        dq = dot(grad_score, kv, ((1,), (0,))) * SCALE
-        od_ref[rows, :] = jnp.where(first, dq, out).astype(jnp.bfloat16)
-        terms = dot(jnp.concatenate([grad_score, rounded], axis=0), diag, ((0,), (0,)))
+        stacked = jnp.concatenate([grad_score, rounded], axis=0)
+        rows_out = dot(stacked, kv, ((1,), (0,)))
+        od_ref[rows, :] = jnp.where(first, rows_out[:BLK] * SCALE, rows_out[BLK:]).astype(jnp.bfloat16)
+        terms = dot(stacked, diag, ((0,), (0,)))
         return picks, terms
 
     def turn(g, carry):
@@ -54,34 +71,36 @@
         return carry
 
     lax.fori_loop(0, local_blocks // group, turn, 0)
-    lane = lax.broadcasted_iota(jnp.int32, (1, PAIR), 1)
-    dkv_ref[...] = (acc[...] * jnp.where(lane < HDIM, SCALE, 1.0)).astype(dkv_ref.dtype)
-
 
 def attention(block_lists, block_counts, qd, kv):
     heads_here, seg_rows, _ = qd.shape
     all_rows = kv.shape[1]
-
-    def spec(rows):
-        kind = {"pipeline_mode": pl.Buffered(1)} if heads_here > 1 else {}
-        return pl.BlockSpec((None, rows, PAIR), lambda h, *_: (h, 0, 0), **kind)
-
+    vmem = pl.BlockSpec(memory_space=pltpu.VMEM)
+    hbm = pl.BlockSpec(memory_space=pltpu.HBM)
+    lists = block_lists.T
+    limit = 6 * MIB + 4 * all_rows * PAIR + 4 * heads_here * (all_rows + seg_rows) * PAIR
     return pl.pallas_call(
-        functools.partial(attention_kernel, math.gcd(2, seg_rows // BLK)),
+        functools.partial(attention_kernel, math.gcd(GROUP, seg_rows // BLK)),
         out_shape=(
-            jax.ShapeDtypeStruct((heads_here, seg_rows, PAIR), jnp.bfloat16),
-            jax.ShapeDtypeStruct((heads_here, all_rows, PAIR), jnp.bfloat16),
+            jax.ShapeDtypeStruct(qd.shape, jnp.bfloat16),
+            jax.ShapeDtypeStruct(kv.shape, jnp.bfloat16),
         ),
-        grid_spec=pltpu.PrefetchScalarGridSpec(
-            num_scalar_prefetch=2,
-            grid=(heads_here,),
-            in_specs=[spec(seg_rows), spec(all_rows)],
-            out_specs=[spec(seg_rows), spec(all_rows)],
-            scratch_shapes=[pltpu.VMEM((all_rows, PAIR), jnp.float32)],
-        ),
-        compiler_params=pltpu.CompilerParams(vmem_limit_bytes=VMEM_BYTES),
+        in_specs=[hbm, hbm, vmem, vmem],
+        out_specs=(vmem, vmem),
+        scratch_shapes=[
+            pltpu.SMEM(lists.shape, jnp.int32),
+            pltpu.SMEM(block_counts.shape, jnp.int32),
+            pltpu.VMEM((all_rows, PAIR), jnp.float32),
+            pltpu.SemaphoreType.DMA((2,)),
+        ],
+        compiler_params=pltpu.CompilerParams(vmem_limit_bytes=limit),
         name="attention",
-    )(block_lists, block_counts, qd, kv)
+    )(
+        pltpu.with_memory_space_constraint(lists, pltpu.HBM),
+        pltpu.with_memory_space_constraint(block_counts, pltpu.HBM),
+        qd,
+        kv,
+    )
 
 
 MESH = pl.DeviceIdType.MESH
@@ -123,8 +142,13 @@
 
 
 def gather_kernel(
-    lanes, q_ref, k_ref, v_ref, g_ref, qd, kv, qd_out, kv_out, qd_s, qd_r, kv_s, kv_r, x_s, x_r, c_s, c_r
+    lanes, q_hbm, k_hbm, v_hbm, g_hbm, qd, kv,
+    k_ref, v_ref, q_ref, g_ref, qd_out, kv_out, in_s, qd_s, qd_r, kv_s, kv_r, x_s, x_r, c_s, c_r,
 ):
+    pairs = ((k_hbm, k_ref), (v_hbm, v_ref), (q_hbm, q_ref), (g_hbm, g_ref))
+    loads = [pltpu.make_async_copy(*pair, in_s.at[n]) for n, pair in enumerate(pairs)]
+    for load in loads:
+        load.start()
     seg, lane, other, across = places()
     heads_here = qd.shape[1]
     barrier = greet(lanes)
@@ -134,6 +158,8 @@
             columns = slice(h * HDIM, (h + 1) * HDIM)
             to[h // heads_here, h % heads_here] = join(left[:, columns], right[:, columns])
 
+    loads[0].wait()
+    loads[1].wait()
     pack(k_ref, v_ref, kv_out)
     pl.semaphore_wait(barrier, lanes + 1)
 
@@ -160,8 +186,9 @@
     kv[seg, lane] = kv_out[lane]
     x_copy(0, lane, seg).start()
     c_copy(0, 0, lane, seg).start()
+    loads[2].wait()
+    loads[3].wait()
     pack(q_ref, g_ref, qd_out)
-    loop(1, lanes, lambda i: qd_copy(i, ahead(i), lane).start())
     qd[lane] = qd_out[lane]
 
     def relay(i):
@@ -171,6 +198,7 @@
     def arrive(i):
         kv_copy(i, lane, behind(i)).wait_recv()
         x_copy(i, behind(i), seg).start()
+        qd_copy(i, ahead(i), lane).start()
         c_copy(0, i, behind(i), seg).start()
         relay(i - 1)
 
@@ -195,8 +223,7 @@
 
 
 def return_kernel(
-    lanes, od, dkv, out_ref, dq_ref, dk_ref, dv_ref,
-    od_in, core_in, x_out, x_in, end_out, end_in,
+    lanes, od, dkv, od_in, end_in, core_in, x_out, x_in, end_out,
     od_s, od_r, c_s, c_r, x_s, x_r, e_s, e_r,
 ):
     seg, lane, other, across = places()
@@ -259,35 +286,36 @@
     loop(lanes + 1 - lag, lanes, reduce_chip)
     end_in[lane] = total(lanes)
 
-    def unpack(block, left, right):
-        for h in range(0, lanes * heads_here, 2):
+    def finish(i):
+        c_copy(0, i, other).wait_send()
+        c_copy(1, i, other).wait_send()
+        x_copy(i).wait_send()
+
+    loop(1, lanes + 1, finish)
+
+    def finish_lanes(i):
+        od_copy(i, lane, behind(i)).wait_recv()
+        end_copy(i, lane, behind(i)).wait_recv()
+        od_copy(i, ahead(i), lane).wait_send()
+        end_copy(i, ahead(i), lane).wait_send()
+
+    loop(1, lanes, finish_lanes)
+
+
+def unpack_kernel(od, dkv, out_ref, dq_ref, dk_ref, dv_ref):
+    for block, left, right in ((od, dq_ref, out_ref), (dkv, dk_ref, dv_ref)):
+        heads_here = block.shape[1]
+        for h in range(0, block.shape[0] * heads_here, 2):
             a, b = (block[g // heads_here, g % heads_here] for g in (h, h + 1))
             columns = slice(h * HDIM, (h + 2) * HDIM)
             left[:, columns] = join(a[:, :HDIM], b[:, :HDIM])
             right[:, columns] = join(a[:, HDIM:], b[:, HDIM:])
 
-    loop(1, lanes, lambda i: od_copy(i, lane, behind(i)).wait_recv())
-    unpack(od_in, dq_ref, out_ref)
-    loop(1, lanes, lambda i: end_copy(i, lane, behind(i)).wait_recv())
-    unpack(end_in, dk_ref, dv_ref)
-
-    def finish(i):
-        c_copy(0, i, other).wait_send()
-        c_copy(1, i, other).wait_send()
-        x_copy(i).wait_send()
-
-    loop(1, lanes + 1, finish)
-
-    def finish_lanes(i):
-        od_copy(i, ahead(i), lane).wait_send()
-        end_copy(i, ahead(i), lane).wait_send()
-
-    loop(1, lanes, finish_lanes)
-
-
-def comm_params(number):
+
+def comm_params(number, chunks, block):
+    chunk_bytes = 2 * math.prod(block)
     return pltpu.CompilerParams(
-        collective_id=number, has_side_effects=True, vmem_limit_bytes=VMEM_BYTES
+        collective_id=number, has_side_effects=True, vmem_limit_bytes=4 * MIB + chunks * chunk_bytes
     )
 
 
@@ -299,21 +327,21 @@
     vmem = pl.BlockSpec(memory_space=pltpu.VMEM)
     dma = pltpu.SemaphoreType.DMA
     half = jnp.bfloat16
+    chunks = jax.ShapeDtypeStruct((lanes, *block), half)
 
     qd, kv = pl.pallas_call(
         functools.partial(gather_kernel, lanes),
-        out_shape=(
-            jax.ShapeDtypeStruct((lanes, *block), half),
-            jax.ShapeDtypeStruct((segs, lanes, *block), half),
-        ),
-        in_specs=[vmem] * 4,
+        out_shape=(chunks, jax.ShapeDtypeStruct((segs, lanes, *block), half)),
+        in_specs=[pl.BlockSpec(memory_space=pltpu.HBM)] * 4,
         out_specs=(vmem, vmem),
-        scratch_shapes=[pltpu.VMEM((lanes, *block), half)] * 2
+        scratch_shapes=[pltpu.VMEM((rows, width), half)] * 4
+        + [pltpu.VMEM((lanes, *block), half)] * 2
+        + [dma((4,))]
         + [dma((lanes,))] * 6
         + [dma((2, lanes))] * 2,
-        compiler_params=comm_params(0),
+        compiler_params=comm_params(0, 10 * lanes, block),
         name="gather",
-    )(query_rows, key_rows, value_rows, out_grad)
+    )(*(pltpu.with_memory_space_constraint(a, pltpu.HBM) for a in (query_rows, key_rows, value_rows, out_grad)))
 
     qd = qd.transpose(1, 0, 2, 3).reshape(heads_here, lanes * rows, PAIR)
     kv = kv.transpose(2, 0, 1, 3, 4).reshape(heads_here, segs * lanes * rows, PAIR)
@@ -321,24 +349,28 @@
     od = od.reshape(heads_here, lanes, rows, PAIR).transpose(1, 0, 2, 3)
     dkv = dkv.reshape(heads_here, segs, lanes, rows, PAIR).transpose(1, 2, 0, 3, 4)
 
-    return tuple(
-        pl.pallas_call(
-            functools.partial(return_kernel, lanes),
-            out_shape=[jax.ShapeDtypeStruct((rows, width), half)] * 4,
-            in_specs=[vmem] * 2,
-            out_specs=[vmem] * 4,
-            scratch_shapes=[
-                pltpu.VMEM((lanes, *block), half),
-                pltpu.VMEM((2, lanes, *block), half),
-            ]
-            + [pltpu.VMEM((lanes, *block), half)] * 4
-            + [dma((lanes + 1,))] * 2
-            + [dma((2, lanes + 1))] * 2
-            + [dma((lanes + 1,))] * 4,
-            compiler_params=comm_params(1),
-            name="scatter",
-        )(od, dkv)
-    )
+    od, dkv = pl.pallas_call(
+        functools.partial(return_kernel, lanes),
+        out_shape=[chunks] * 2,
+        in_specs=[vmem] * 2,
+        out_specs=[vmem] * 2,
+        scratch_shapes=[pltpu.VMEM((2, lanes, *block), half)]
+        + [pltpu.VMEM((lanes, *block), half)] * 3
+        + [dma((lanes + 1,))] * 2
+        + [dma((2, lanes + 1))] * 2
+        + [dma((lanes + 1,))] * 4,
+        compiler_params=comm_params(1, 14 * lanes, block),
+        name="scatter",
+    )(od, dkv)
+
+    return pl.pallas_call(
+        unpack_kernel,
+        out_shape=[jax.ShapeDtypeStruct((rows, width), half)] * 4,
+        in_specs=[vmem] * 2,
+        out_specs=[vmem] * 4,
+        compiler_params=pltpu.CompilerParams(vmem_limit_bytes=4 * MIB + 32 * rows * width),
+        name="unpack",
+    )(od, dkv)
 
 
 def solution(mesh):

time: 67 us -> 50.4 us (0.75)
  Pallas kernels: 60.5 us -> 49.5 us
  local copies, waits for them, and re-layouts: 5.52 us -> 0 us
    pallas_call x3 -> x4, Pallas kernels: 60.5 us -> 49.5 us  [the longest x1 23.5 us: on_device(): pl.pallas_call(functools.partial(gather_kernel, lanes), out_shape=(chunks...]
    unnamed x11 -> x0, local copies, waits for them, and re-layouts: 5.52 us -> none
where the time goes in v3:
time: 50.4 us; the launch traced here: 50.2 us
  Pallas kernels  49.5 us (98%)
  between operations  0.66 us (1%)
    pallas_call x1, Pallas kernels, on_device(): pl.pallas_call(functools.partial(gather_kernel, lanes), out_shape=(chunks...  23.5 us
    pallas_call x1, Pallas kernels, on_device(): pl.pallas_call(functools.partial(return_kernel, lanes), out_shape=[chunks...  16.5 us
    pallas_call x1, Pallas kernels, attention(): pl.pallas_call(functools.partial(attention_kernel, math.gcd(GROUP, seg_ro...  8.6 us

profile of v3, /device:TPU:0, one launch (start us, length us, event | category | flops | bytes accessed | tf_op | source)
XLA Modules:
  0.0 50.2 jit_solution(6283446140339675227)
XLA Ops:
  0.6 23.5 %gather.1 = (bf16[8,1,128,128]{3,2,1,0:T(8,128)(2,1)S(1)}, bf16[4,8,1,128,128]{4,3,2,1,0:T(8,128)(2,1)S(1)}) custom-call(bf16[128,512]{1,0:T(8,128)(2,1)} %q_hbm.1, bf16[128,512]{1,0:T(8,128)(2,1)} %k_hbm.1, bf16[128,512]{1,0:T(8,128)(2,1)} %v_hbm.1, bf16[128,512]{1,0:T(8,128)(2,1)} %g_hbm.1), custom_call_target="tpu_custom_call" | custom-call | tf_op jit(solution)/shard_map/gather/pallas_call | solution.py:332
  24.2 8.6 %attention.1 = (bf16[1,1024,128]{2,1,0:T(8,128)(2,1)S(1)}, bf16[1,4096,128]{2,1,0:T(8,128)(2,1)S(1)}) custom-call(s32[8,16]{1,0:T(8,128)} %bitcast.9, s32[16]{0:T(128)} %counts_hbm.1, bf16[1,1024,128]{2,1,0:T(8,128)(2,1)S(1)} %bitcast.8, bf16[1,4096,128]{2,1,0:T(8,128)(2,1)S(1)} %bitcast.6), custom_call_target="tpu_custom_call" | custom-call | tf_op jit(solution)/shard_map/attention/pallas_call | solution.py:82
  32.8 16.5 %scatter.1 = (bf16[8,1,128,128]{3,2,1,0:T(8,128)(2,1)S(1)}, bf16[8,1,128,128]{3,2,1,0:T(8,128)(2,1)S(1)}) custom-call(bf16[8,1,128,128]{3,2,1,0:T(8,128)(2,1)S(1)} %bitcast.7, bf16[4,8,1,128,128]{4,3,2,1,0:T(8,128)(2,1)S(1)} %bitcast.5), custom_call_target="tpu_custom_call" | custom-call | tf_op jit(solution)/shard_map/scatter/pallas_call | solution.py:352
  49.3 0.9 %unpack.1 = (bf16[128,512]{1,0:T(8,128)(2,1)}, bf16[128,512]{1,0:T(8,128)(2,1)}, bf16[128,512]{1,0:T(8,128)(2,1)}, bf16[128,512]{1,0:T(8,128)(2,1)}) custom-call(bf16[8,1,128,128]{3,2,1,0:T(8,128)(2,1)S(1)} %get-tuple-element.14.od, bf16[8,1,128,128]{3,2,1,0:T(8,128)(2,1)S(1)} %get-tuple-element.15.dkv), custom_call_target="tpu_custom_call" | custom-call | tf_op jit(solution)/shard_map/unpack/pallas_call | solution.py:366

commit v4 on v3

--- a/solution.py
+++ b/solution.py
@@ -13,7 +13,7 @@
 KSEL = 8
 PAIR = 2 * HDIM
 SCALE = 1.0 / math.sqrt(HDIM)
-GROUP = 8
+GROUP = 16
 MIB = 1024 * 1024
 
 
@@ -118,7 +118,7 @@
     )
 
 
-def greet(lanes):
+def greet(lanes, diagonal=False):
     seg, lane, other, across = places()
     barrier = pltpu.get_barrier_semaphore()
 
@@ -128,7 +128,7 @@
         return carry
 
     lax.fori_loop(1, lanes, one, 0)
-    for near in (other, across):
+    for near in (other, across, lax.rem(other + 2, 4))[: 3 if diagonal else 2]:
         pl.semaphore_signal(barrier, inc=1, device_id=(near, lane), device_id_type=MESH)
     return barrier
 
@@ -151,7 +151,7 @@
         load.start()
     seg, lane, other, across = places()
     heads_here = qd.shape[1]
-    barrier = greet(lanes)
+    barrier = greet(lanes, True)
 
     def pack(left, right, to):
         for h in range(lanes * heads_here):
@@ -161,7 +161,7 @@
     loads[0].wait()
     loads[1].wait()
     pack(k_ref, v_ref, kv_out)
-    pl.semaphore_wait(barrier, lanes + 1)
+    pl.semaphore_wait(barrier, lanes + 2)
 
     def kv_copy(i, target, source):
         return remote(kv_out.at[target], kv.at[seg, source], kv_s.at[i], kv_r.at[i], (seg, target))
@@ -174,7 +174,8 @@
 
     def c_copy(n, i, source, whose):
         block = kv.at[whose, source]
-        return remote(block, block, c_s.at[n, i], c_r.at[n, i], (other, lane))
+        near = other if n == 0 else lax.rem(other + 2, 4)
+        return remote(block, block, c_s.at[n, i], c_r.at[n, i], (near, lane))
 
     def ahead(i):
         return lax.rem(lane + i, lanes)
@@ -185,32 +186,29 @@
     loop(1, lanes, lambda i: kv_copy(i, ahead(i), lane).start())
     kv[seg, lane] = kv_out[lane]
     x_copy(0, lane, seg).start()
+    c_copy(1, 0, lane, seg).start()
     c_copy(0, 0, lane, seg).start()
     loads[2].wait()
     loads[3].wait()
     pack(q_ref, g_ref, qd_out)
     qd[lane] = qd_out[lane]
 
-    def relay(i):
-        x_copy(i, behind(i), across).wait_recv()
-        c_copy(1, i, behind(i), across).start()
-
     def arrive(i):
         kv_copy(i, lane, behind(i)).wait_recv()
         x_copy(i, behind(i), seg).start()
         qd_copy(i, ahead(i), lane).start()
+        c_copy(1, i, behind(i), seg).start()
         c_copy(0, i, behind(i), seg).start()
-        relay(i - 1)
 
     loop(1, lanes, arrive)
-    relay(lanes - 1)
+    loop(0, lanes, lambda i: x_copy(i, behind(i), across).wait_recv())
 
     def finish(i):
         c_copy(0, i, behind(i), other).wait_recv()
         c_copy(1, i, behind(i), lax.rem(other + 2, 4)).wait_recv()
         x_copy(i, behind(i), seg).wait_send()
         c_copy(0, i, behind(i), seg).wait_send()
-        c_copy(1, i, behind(i), across).wait_send()
+        c_copy(1, i, behind(i), seg).wait_send()
 
     loop(0, lanes, finish)
 

time: 50.4 us -> 47.3 us (0.938)
  Pallas kernels: 49.5 us -> 46.5 us
    pallas_call x1, Pallas kernels: 23.5 us -> 20.8 us  [on_device(): pl.pallas_call(functools.partial(gather_kernel, lanes), out_shape=(chunks...]
where the time goes in v4:
time: 47.3 us; the launch traced here: 47.1 us
  Pallas kernels  46.5 us (98%)
  between operations  0.66 us (1%)
    pallas_call x1, Pallas kernels, on_device(): pl.pallas_call(functools.partial(gather_kernel, lanes), out_shape=(chunks...  20.8 us
    pallas_call x1, Pallas kernels, on_device(): pl.pallas_call(functools.partial(return_kernel, lanes), out_shape=[chunks...  16.3 us
    pallas_call x1, Pallas kernels, attention(): pl.pallas_call(functools.partial(attention_kernel, math.gcd(GROUP, seg_ro...  8.44 us

profile of v4, /device:TPU:0, one launch (start us, length us, event | category | flops | bytes accessed | tf_op | source)
XLA Modules:
  0.0 47.1 jit_solution(11821628966841707990)
XLA Ops:
  0.6 20.8 %gather.1 = (bf16[8,1,128,128]{3,2,1,0:T(8,128)(2,1)S(1)}, bf16[4,8,1,128,128]{4,3,2,1,0:T(8,128)(2,1)S(1)}) custom-call(bf16[128,512]{1,0:T(8,128)(2,1)} %q_hbm.1, bf16[128,512]{1,0:T(8,128)(2,1)} %k_hbm.1, bf16[128,512]{1,0:T(8,128)(2,1)} %v_hbm.1, bf16[128,512]{1,0:T(8,128)(2,1)} %g_hbm.1), custom_call_target="tpu_custom_call" | custom-call | tf_op jit(solution)/shard_map/gather/pallas_call | solution.py:330
  21.4 8.4 %attention.1 = (bf16[1,1024,128]{2,1,0:T(8,128)(2,1)S(1)}, bf16[1,4096,128]{2,1,0:T(8,128)(2,1)S(1)}) custom-call(s32[8,16]{1,0:T(8,128)} %bitcast.9, s32[16]{0:T(128)} %counts_hbm.1, bf16[1,1024,128]{2,1,0:T(8,128)(2,1)S(1)} %bitcast.8, bf16[1,4096,128]{2,1,0:T(8,128)(2,1)S(1)} %bitcast.6), custom_call_target="tpu_custom_call" | custom-call | tf_op jit(solution)/shard_map/attention/pallas_call | solution.py:82
  29.9 16.3 %scatter.1 = (bf16[8,1,128,128]{3,2,1,0:T(8,128)(2,1)S(1)}, bf16[8,1,128,128]{3,2,1,0:T(8,128)(2,1)S(1)}) custom-call(bf16[8,1,128,128]{3,2,1,0:T(8,128)(2,1)S(1)} %bitcast.7, bf16[4,8,1,128,128]{4,3,2,1,0:T(8,128)(2,1)S(1)} %bitcast.5), custom_call_target="tpu_custom_call" | custom-call | tf_op jit(solution)/shard_map/scatter/pallas_call | solution.py:350
  46.2 0.9 %unpack.1 = (bf16[128,512]{1,0:T(8,128)(2,1)}, bf16[128,512]{1,0:T(8,128)(2,1)}, bf16[128,512]{1,0:T(8,128)(2,1)}, bf16[128,512]{1,0:T(8,128)(2,1)}) custom-call(bf16[8,1,128,128]{3,2,1,0:T(8,128)(2,1)S(1)} %get-tuple-element.14.od, bf16[8,1,128,128]{3,2,1,0:T(8,128)(2,1)S(1)} %get-tuple-element.15.dkv), custom_call_target="tpu_custom_call" | custom-call | tf_op jit(solution)/shard_map/unpack/pallas_call | solution.py:364

commit v5 on v4

--- a/solution.py
+++ b/solution.py
@@ -269,7 +269,7 @@
         end_out[ahead(i)] = total(i)
         end_copy(i, ahead(i), lane).start()
 
-    lag = min(2, lanes - 1)
+    lag = min(4, lanes - 1)
     pl.semaphore_wait(barrier, lanes + 1)
     loop(1, lanes + 1, send)
     loop(1, lanes, lambda i: od_copy(i, ahead(i), lane).start())

time: 47.3 us -> 46.5 us (0.983)
  Pallas kernels: 46.5 us -> 45.7 us
    pallas_call x1, Pallas kernels: 16.3 us -> 15.5 us  [on_device(): pl.pallas_call(functools.partial(return_kernel, lanes), out_shape=[chunks...]
where the time goes in v5:
time: 46.5 us; the launch traced here: 46.3 us
  Pallas kernels  45.7 us (98%)
  between operations  0.66 us (1%)
    pallas_call x1, Pallas kernels, on_device(): pl.pallas_call(functools.partial(gather_kernel, lanes), out_shape=(chunks...  20.8 us
    pallas_call x1, Pallas kernels, on_device(): pl.pallas_call(functools.partial(return_kernel, lanes), out_shape=[chunks...  15.5 us
    pallas_call x1, Pallas kernels, attention(): pl.pallas_call(functools.partial(attention_kernel, math.gcd(GROUP, seg_ro...  8.46 us

profile of v5, /device:TPU:0, one launch (start us, length us, event | category | flops | bytes accessed | tf_op | source)
XLA Modules:
  0.0 46.3 jit_solution(17710484610363360458)
XLA Ops:
  0.6 20.8 %gather.1 = (bf16[8,1,128,128]{3,2,1,0:T(8,128)(2,1)S(1)}, bf16[4,8,1,128,128]{4,3,2,1,0:T(8,128)(2,1)S(1)}) custom-call(bf16[128,512]{1,0:T(8,128)(2,1)} %q_hbm.1, bf16[128,512]{1,0:T(8,128)(2,1)} %k_hbm.1, bf16[128,512]{1,0:T(8,128)(2,1)} %v_hbm.1, bf16[128,512]{1,0:T(8,128)(2,1)} %g_hbm.1), custom_call_target="tpu_custom_call" | custom-call | tf_op jit(solution)/shard_map/gather/pallas_call | solution.py:330
  21.4 8.5 %attention.1 = (bf16[1,1024,128]{2,1,0:T(8,128)(2,1)S(1)}, bf16[1,4096,128]{2,1,0:T(8,128)(2,1)S(1)}) custom-call(s32[8,16]{1,0:T(8,128)} %bitcast.9, s32[16]{0:T(128)} %counts_hbm.1, bf16[1,1024,128]{2,1,0:T(8,128)(2,1)S(1)} %bitcast.8, bf16[1,4096,128]{2,1,0:T(8,128)(2,1)S(1)} %bitcast.6), custom_call_target="tpu_custom_call" | custom-call | tf_op jit(solution)/shard_map/attention/pallas_call | solution.py:82
  29.9 15.5 %scatter.1 = (bf16[8,1,128,128]{3,2,1,0:T(8,128)(2,1)S(1)}, bf16[8,1,128,128]{3,2,1,0:T(8,128)(2,1)S(1)}) custom-call(bf16[8,1,128,128]{3,2,1,0:T(8,128)(2,1)S(1)} %bitcast.7, bf16[4,8,1,128,128]{4,3,2,1,0:T(8,128)(2,1)S(1)} %bitcast.5), custom_call_target="tpu_custom_call" | custom-call | tf_op jit(solution)/shard_map/scatter/pallas_call | solution.py:350
  45.4 0.9 %unpack.1 = (bf16[128,512]{1,0:T(8,128)(2,1)}, bf16[128,512]{1,0:T(8,128)(2,1)}, bf16[128,512]{1,0:T(8,128)(2,1)}, bf16[128,512]{1,0:T(8,128)(2,1)}) custom-call(bf16[8,1,128,128]{3,2,1,0:T(8,128)(2,1)S(1)} %get-tuple-element.14.od, bf16[8,1,128,128]{3,2,1,0:T(8,128)(2,1)S(1)} %get-tuple-element.15.dkv), custom_call_target="tpu_custom_call" | custom-call | tf_op jit(solution)/shard_map/unpack/pallas_call | solution.py:364
